TPU v7x, 256 devices: a whole 4x4x8 slice. The times are simulated.
256 devices in a mesh: node: 16 (over x, z_hi), tm: 16 (over z_lo, y, core).
Axes of the slice: x: 4, y: 4, z: 8 (z_hi: 4, z_lo: 2; z = z_hi * 2 + z_lo), core: 2. Of those that a mesh axis runs over, the one named last changes fastest.
Arguments:
- codes: int32 [65536, 2048], P('node', 'tm'), may hold values from -127 to 127
- node_scale: float32 [65536], P('node'), may hold values from 0.002 to 0.02
- basis: bfloat16 [65536, 128], P('node'), may hold values from -0.0234375 to 0.0234375
- regular: float32 [8384], replicated, may hold values from 0.05 to 0.5
- feature_order: int32 [8384], replicated, may hold values from 0 to 8383, each once
- panel_inverse: float32 [2, 262, 262], replicated, may hold values from -0.06 to 1.2
Outputs:
- schur: float32 [8384, 8384], P('node', 'tm')
Inputs may be any that keep to these rules, and one draw needn't show every extreme that they name: `feature_order`: a permutation: every feature stands at exactly one position.
All inputs are finite; a program needn't handle non-finite values.
Results may differ from a plain program's by a relative error of at most 0.0051.
Values sent between devices are 32-bit elements; how exact they have to be, the bound alone decides.
A program may use at most 64 MiB of HBM per device.

v0:
```python
import jax
import jax.numpy as jnp
import numpy as np
from jax import lax
from jax.sharding import PartitionSpec as P


def pair_starts(rank_count):
    leading = np.arange(rank_count + 1)
    return (leading * (rank_count + 1) - leading * (leading - 1) // 2).astype(np.int32)


def selectors(chosen, rank_count):
    starts = pair_starts(rank_count)
    modes = jnp.arange(rank_count, dtype=jnp.int32)
    below = chosen[:, None] >= jnp.asarray(starts[:-1])[None, :]
    above = chosen[:, None] < jnp.asarray(starts[1:])[None, :]
    lead = jnp.logical_and(below, above)
    shift = modes - jnp.asarray(starts[:-1])
    trailing = chosen + jnp.sum(jnp.where(lead, shift[None, :], 0), axis=1)
    trail = trailing[:, None] == modes[None, :]
    keep = (trailing < rank_count).astype(jnp.float32)
    return (lead.astype(jnp.bfloat16), trail.astype(jnp.bfloat16), 1.0 - keep)


def spread(values):
    high = lax.reduce_precision(values, 8, 7)
    low = lax.reduce_precision(values - high, 8, 7)
    return jnp.concatenate([high, low], axis=1).astype(jnp.bfloat16)


def make_features(pieces, picks):
    lead, trail, constant = picks
    dims = (((1,), (1,)), ((), ()))
    lead = jnp.concatenate([lead, lead], axis=1)
    trail = jnp.concatenate([trail, trail], axis=1)
    lead_vals = lax.dot_general(lead, pieces, dims, preferred_element_type=jnp.float32)
    trail_vals = lax.dot_general(trail, pieces, dims, preferred_element_type=jnp.float32)
    return (lead_vals * (trail_vals + constant[:, None])).astype(jnp.bfloat16)


def contract(left_feats, right_feats):
    return lax.dot_general(
        left_feats, right_feats, (((1,), (1,)), ((), ())), preferred_element_type=jnp.float32
    )


def highest(left_mat, right_mat):
    return jnp.dot(
        left_mat, right_mat, precision=lax.Precision.HIGHEST, preferred_element_type=jnp.float32
    )


def per_device(codes, node_scale, basis, regular, feature_order, panel_inverse):
    rank_count = basis.shape[1]
    snap_local = codes.shape[1]
    nfeat = regular.shape[0]
    row_size = nfeat // lax.axis_size("node")
    col_size = nfeat // lax.axis_size("tm")
    snap_total = snap_local * lax.axis_size("tm")
    panel_width = panel_inverse.shape[1]
    span = 2 * panel_width
    scaled_basis = (basis.astype(jnp.float32) * node_scale[:, None]).astype(jnp.bfloat16)
    code_values = codes.astype(jnp.bfloat16)
    row_offset = lax.axis_index("node") * row_size
    col_offset = lax.axis_index("tm") * col_size
    row_picks = selectors(lax.dynamic_slice_in_dim(feature_order, row_offset, row_size), rank_count)
    col_picks = selectors(lax.dynamic_slice_in_dim(feature_order, col_offset, col_size), rank_count)
    pan_picks = selectors(feature_order[:span], rank_count)
    summed = lax.psum(
        lax.dot_general(
            code_values, scaled_basis, (((0,), (0,)), ((), ())), preferred_element_type=jnp.float32
        ),
        "node",
    )
    pieces = spread(lax.all_gather(summed, "tm", axis=0, tiled=True))
    row_feats = make_features(pieces, row_picks)
    col_feats = make_features(pieces, col_picks)
    pan_feats = make_features(pieces, pan_picks)
    row_global = row_offset + jnp.arange(row_size, dtype=jnp.int32)
    col_global = col_offset + jnp.arange(col_size, dtype=jnp.int32)
    pan_global = jnp.arange(span, dtype=jnp.int32)
    row_regular = lax.dynamic_slice_in_dim(regular, row_offset, row_size)

    def block(left_feats, right_feats, left_global, right_global, left_regular):
        same = (left_global[:, None] == right_global[None, :]).astype(jnp.float32)
        return contract(left_feats, right_feats) / snap_total + same * left_regular[:, None]

    matrix = block(row_feats, col_feats, row_global, col_global, row_regular)
    left = block(row_feats, pan_feats, row_global, pan_global, row_regular)
    upper = block(pan_feats, col_feats, pan_global, col_global, regular[:span])
    w = panel_width
    inner = contract(pan_feats[:w], pan_feats[w:]) / snap_total
    first_left = highest(left[:, :w], panel_inverse[0])
    second_left = left[:, w:] - highest(first_left, inner)
    cross = highest(panel_inverse[0], inner)
    second_upper = upper[w:] - highest(cross.T, upper[:w])
    second_left = highest(second_left, panel_inverse[1])
    joint = jnp.concatenate([first_left, second_left], axis=1)
    return matrix - highest(joint, jnp.concatenate([upper[:w], second_upper], axis=0))


def solution(mesh):
    placed = (P("node", "tm"), P("node"), P("node", None), P(), P(), P())
    return jax.shard_map(
        per_device, mesh=mesh, in_specs=placed, out_specs=P("node", "tm"), check_vma=False
    )
```

profile of v0, /device:TPU:1, one launch (start us, length us, event | category | flops | bytes accessed | tf_op | source)
XLA Modules:
  0.0 236.5 jit_solution(14011582777847682140)
XLA Ops:
  6.5 0.0 copy-start.1
  6.5 0.0 copy-start.2
  6.5 0.0 copy-start.3
  6.5 0.0 copy-start
  6.5 0.0 all-reduce.2.cloned.1.call-start
  6.6 3.7 %convolution_bitcast_fusion = f32[128,128]{0,1:T(8,128)} fusion(bf16[4096,128]{1,0:T(8,128)(2,1)} %param.17, s32[4096,128]{1,0:T(8,128)} %param.15, f32[4096]{0:T(1024)} %param.16), kind=kOutput, calls=%fused_computation.24 | convolution fusion | flops 136314880 | bytes 3227648 | tf_op jit(solution)/shard_map/dot_general | solution.py:71
  10.3 0.0 all-reduce.2.cloned.1.call-update
  10.3 0.0 all-gather.2.cloned.1.call-start
  10.4 0.9 fusion.50
  11.3 147.1 %all-reduce.2.cloned.1.call-done = f32[128,128]{0,1:T(8,128)} async-done(((f32[128,128]{0,1:T(8,128)}), f32[128,128]{0,1:T(8,128)}) %all-reduce.2.cloned.1.call-update) | async-done | bytes 65552 | tf_op jit(solution)/shard_map/psum | solution.py:70
  158.3 0.0 all-gather.2.cloned.1.call-update
  158.3 0.0 copy-done.1
  158.3 0.0 copy-done.2
  158.4 0.0 copy-done.3
  158.4 0.6 select_reduce_fusion
  159.0 0.9 fusion.49
  159.8 0.7 convert_subtract_fusion
  160.5 0.1 iota_compare_fusion.4
  160.6 0.1 iota_compare_fusion.3
  160.8 0.1 iota_compare_fusion.2
  160.9 0.3 compare_and_fusion
  161.2 0.0 copy-done
  161.2 0.6 fusion.48
  161.9 41.1 %all-gather.2.cloned.1.call-done = f32[2048,128]{0,1:T(8,128)} async-done(((f32[128,128]{0,1:T(8,128)}), f32[2048,128]{0,1:T(8,128)}) %all-gather.2.cloned.1.call-update) | async-done | bytes 1048592 | tf_op jit(solution)/shard_map/all_gather | solution.py:76
  202.9 1.4 reduce-precision_convert_fusion
  204.3 0.7 fusion.17
  205.1 0.7 fusion.24
  205.8 0.7 fusion.31
  206.5 0.9 multiply_convert_fusion
  207.4 0.8 convolution_multiply_fusion.3
  208.2 0.8 multiply_convert_fusion.2
  209.0 2.0 fusion.1
  211.0 1.6 fusion.15
  212.6 1.9 fusion.39
  214.5 2.2 convolution_subtract_fusion.1
  216.7 0.8 multiply_convert_fusion.1
  217.5 1.9 fusion
  219.4 1.9 fusion.2
  221.3 1.5 convolution_subtract_fusion.2
  222.8 1.6 fusion.38
  224.4 5.2 %convolution_subtract_fusion = f32[524,524]{1,0:T(8,128)} fusion(f32[524,524]{1,0:T(8,128)S(1)} %fusion, f32[524,262]{0,1:T(8,128)S(1)} %fusion.38, f32[524,262]{0,1:T(8,128)S(1)} %fusion.15, f32[262,524]{1,0:T(8,128)S(1)} %convolution_subtract_fusion.2, f32[262,524]{1,0:T(8,128)S(1)} %slice.46), kind=kOutput, calls=%fused_computation.6 | convolution fusion | flops 1727357696 | bytes 4393216 | tf_op jit(solution)/shard_map/dot_general | solution.py:49
  (3 shorter events, 0.1 us)
Async XLA Ops:
  6.5 151.8 %copy-start.1 = (s32[128]{0:T(128)S(1)}, s32[128]{0:T(128)}, u32[]{:S(2)}) copy-start(s32[128]{0:T(128)} %constant.33.clone) | copy-start | bytes 1540
  6.5 151.8 %copy-start.2 = (s32[128]{0:T(128)S(1)}, s32[128]{0:T(128)}, u32[]{:S(2)}) copy-start(s32[128]{0:T(128)} %constant.32.clone) | copy-start | bytes 1540
  6.5 151.8 %copy-start.3 = (s32[128]{0:T(128)S(1)}, s32[128]{0:T(128)}, u32[]{:S(2)}) copy-start(s32[128]{0:T(128)} %constant.35) | copy-start | bytes 1540
  6.5 154.7 %copy-start = (f32[2,262,262]{2,0,1:T(2,128)S(1)}, f32[2,262,262]{2,0,1:T(2,128)}, u32[]{:S(2)}) copy-start(f32[2,262,262]{2,0,1:T(2,128)} %param.20) | copy-start | bytes 1647460
  6.5 151.8 %all-reduce.2.cloned.1.call-start = ((), (), s32[]{:S(2)}) async-start(), calls=%async_computation | async-start | bytes 131072 | tf_op jit(solution)/shard_map/psum | solution.py:70
  10.3 192.6 %all-gather.2.cloned.1.call-start = ((), (), s32[]{:S(2)}) async-start(), calls=%async_computation.1 | async-start | bytes 1114112 | tf_op jit(solution)/shard_map/all_gather | solution.py:76
Sparse Core Ops, SparseCore 0:
  10.4 147.8 all-reduce.1
  160.2 42.6 all-gather.1
where the time goes:
time: 237 us; the launch traced here: 236 us
  waiting for transfers between devices  188 us (79%)
  matrix products  28.9 us (12%)
  between operations  13.6 us (6%)
  other arithmetic  3.34 us (1%)
  local copies, waits for them, and re-layouts  2.42 us (1%)
    psum x1, waiting for transfers between devices, per_device(): lax.psum(lax.dot_general(code_values, scaled_basis, (((0,), (0,)), ((), (...  147 us
    all_gather x1, waiting for transfers between devices, per_device(): pieces = spread(lax.all_gather(summed, 'tm', axis=0, tiled=True))  41.1 us
    dot_general x6, matrix products, highest(): jnp.dot(left_mat, right_mat, precision=lax.Precision.HIGHEST, preferred_e...  14 us
    dot_general x4, matrix products, contract(): lax.dot_general(left_feats, right_feats, (((1,), (1,)), ((), ())), prefer...  6.5 us
  transfers between devices with their start and end apart: 2, of which 2 were waited for; matrix products, arithmetic and copies ran while one was open for 2% of the time, Pallas kernels for 0%

commit v1 on v0

--- a/solution.py
+++ b/solution.py
@@ -3,6 +3,13 @@
 import numpy as np
 from jax import lax
 from jax.sharding import PartitionSpec as P
+
+
+def swapped_in(x, axis, dim):
+    count = lax.axis_size(axis)
+    blocks = jnp.stack([x for _ in range(count)])
+    blocks = lax.all_to_all(blocks, axis, split_axis=0, concat_axis=0)
+    return jnp.concatenate(blocks, axis=dim)
 
 
 def pair_starts(rank_count):
@@ -73,7 +80,7 @@
         ),
         "node",
     )
-    pieces = spread(lax.all_gather(summed, "tm", axis=0, tiled=True))
+    pieces = spread(swapped_in(summed, "tm", 0))
     row_feats = make_features(pieces, row_picks)
     col_feats = make_features(pieces, col_picks)
     pan_feats = make_features(pieces, pan_picks)

time: 237 us -> 224 us (0.945)
  waiting for transfers between devices: 188 us -> 159 us
  starting transfers between devices: 0.08 us -> 14.9 us
    all_gather x1 -> x0, waiting for transfers between devices: 41.1 us -> none  [per_device(): pieces = spread(lax.all_gather(summed, 'tm', axis=0, tiled=True))]
    all_to_all x0 -> x1, starting transfers between devices: none -> 14.9 us  [swapped_in(): blocks = lax.all_to_all(blocks, axis, split_axis=0, concat_axis=0)]
    all_to_all x0 -> x1, waiting for transfers between devices: none -> 12.3 us  [swapped_in(): blocks = lax.all_to_all(blocks, axis, split_axis=0, concat_axis=0)]
where the time goes in v1:
time: 224 us; the launch traced here: 223 us
  waiting for transfers between devices  159 us (71%)
  matrix products  28.8 us (13%)
  starting transfers between devices  14.9 us (7%)
  between operations  13.6 us (6%)
  local copies, waits for them, and re-layouts  4.42 us (2%)
    psum x1, waiting for transfers between devices, per_device(): lax.psum(lax.dot_general(code_values, scaled_basis, (((0,), (0,)), ((), (...  147 us
    all_to_all x1, starting transfers between devices, swapped_in(): blocks = lax.all_to_all(blocks, axis, split_axis=0, concat_axis=0)  14.9 us
    dot_general x6, matrix products, highest(): jnp.dot(left_mat, right_mat, precision=lax.Precision.HIGHEST, preferred_e...  14 us
    all_to_all x1, waiting for transfers between devices, swapped_in(): blocks = lax.all_to_all(blocks, axis, split_axis=0, concat_axis=0)  12.3 us
    dot_general x4, matrix products, contract(): lax.dot_general(left_feats, right_feats, (((1,), (1,)), ((), ())), prefer...  6.4 us
  transfers between devices with their start and end apart: 2, of which 2 were waited for; matrix products, arithmetic and copies ran while one was open for 2% of the time, Pallas kernels for 0%

profile of v1, /device:TPU:1, one launch (start us, length us, event | category | flops | bytes accessed | tf_op | source)
XLA Modules:
  0.0 223.3 jit_solution(11627700104859935925)
XLA Ops:
  6.5 0.0 all-reduce.2.cloned.1.call-start
  6.5 3.6 %convolution_bitcast_fusion = f32[128,128]{0,1:T(8,128)} fusion(bf16[4096,128]{1,0:T(8,128)(2,1)} %param.17, s32[4096,128]{1,0:T(8,128)} %param.15, f32[4096]{0:T(1024)} %param.16), kind=kOutput, calls=%fused_computation.24 | convolution fusion | flops 136314880 | bytes 3227648 | tf_op jit(solution)/shard_map/dot_general | solution.py:78
  10.2 0.0 copy-start.1
  10.2 0.0 copy-start.2
  10.2 0.0 copy-start.3
  10.2 0.0 copy-start
  10.2 0.0 all-reduce.2.cloned.1.call-update
  10.2 0.9 fusion.50
  11.1 147.1 %all-reduce.2.cloned.1.call-done = f32[128,128]{0,1:T(8,128)} async-done(((f32[128,128]{0,1:T(8,128)}), f32[128,128]{0,1:T(8,128)}) %all-reduce.2.cloned.1.call-update) | async-done | bytes 65552 | tf_op jit(solution)/shard_map/psum | solution.py:77
  158.2 0.9 copy.22
  159.2 1.1 stack.2
  160.2 14.9 %all-to-all-start = ((f32[16,128,128]{2,1,0:T(8,128)}), f32[16,128,128]{2,1,0:T(8,128)S(1)}, u32[]{:S(2)}, u32[]{:S(2)}) async-start(f32[16,128,128]{2,1,0:T(8,128)} %stack.2), calls=%async_computation | async-start | bytes 2097152 | tf_op jit(solution)/shard_map/all_to_all | solution.py:11
  175.1 0.0 copy-done.1
  175.1 0.0 copy-done.2
  175.1 0.0 copy-done.3
  175.1 0.6 select_reduce_fusion
  175.7 0.9 fusion.49
  176.6 0.7 convert_subtract_fusion
  177.3 0.1 iota_compare_fusion.4
  177.4 0.1 iota_compare_fusion.3
  177.6 0.1 iota_compare_fusion.2
  177.7 0.3 compare_and_fusion
  178.0 0.0 copy-done
  178.0 0.6 fusion.48
  178.6 12.3 %all-to-all-done = f32[16,128,128]{2,1,0:T(8,128)S(1)} async-done(((f32[16,128,128]{2,1,0:T(8,128)}), f32[16,128,128]{2,1,0:T(8,128)S(1)}, u32[]{:S(2)}, u32[]{:S(2)}) %all-to-all-start) | async-done | bytes 1048608 | tf_op jit(solution)/shard_map/all_to_all | solution.py:11
  191.0 0.2 reduce-precision_convert_fusion
  191.1 0.8 fusion.17
  191.9 0.8 fusion.24
  192.7 0.8 fusion.31
  193.5 0.8 multiply_convert_fusion
  194.3 0.8 convolution_multiply_fusion.3
  195.1 0.8 multiply_convert_fusion.2
  195.9 1.9 fusion.1
  197.8 1.6 fusion.15
  199.4 1.9 fusion.39
  201.3 2.2 convolution_subtract_fusion.1
  203.5 0.8 multiply_convert_fusion.1
  204.3 1.9 fusion
  206.2 1.9 fusion.2
  208.1 1.5 convolution_subtract_fusion.2
  209.6 1.6 fusion.38
  211.2 5.2 %convolution_subtract_fusion = f32[524,524]{1,0:T(8,128)} fusion(f32[524,524]{1,0:T(8,128)S(1)} %fusion, f32[524,262]{0,1:T(8,128)S(1)} %fusion.38, f32[524,262]{0,1:T(8,128)S(1)} %fusion.15, f32[262,524]{1,0:T(8,128)S(1)} %convolution_subtract_fusion.2, f32[262,524]{1,0:T(8,128)S(1)} %slice.46), kind=kOutput, calls=%fused_computation.6 | convolution fusion | flops 1727357696 | bytes 4393216 | tf_op jit(solution)/shard_map/dot_general | solution.py:56
  (3 shorter events, 0.1 us)
Async XLA Ops:
  6.5 151.7 %all-reduce.2.cloned.1.call-start = ((), (), s32[]{:S(2)}) async-start(), calls=%async_computation.1 | async-start | bytes 131072 | tf_op jit(solution)/shard_map/psum | solution.py:77
  10.2 164.9 %copy-start.1 = (s32[128]{0:T(128)S(1)}, s32[128]{0:T(128)}, u32[]{:S(2)}) copy-start(s32[128]{0:T(128)} %constant.33.clone) | copy-start | bytes 1540
  10.2 164.9 %copy-start.2 = (s32[128]{0:T(128)S(1)}, s32[128]{0:T(128)}, u32[]{:S(2)}) copy-start(s32[128]{0:T(128)} %constant.32.clone) | copy-start | bytes 1540
  10.2 164.9 %copy-start.3 = (s32[128]{0:T(128)S(1)}, s32[128]{0:T(128)}, u32[]{:S(2)}) copy-start(s32[128]{0:T(128)} %constant.35) | copy-start | bytes 1540
  10.2 167.8 %copy-start = (f32[2,262,262]{2,0,1:T(2,128)S(1)}, f32[2,262,262]{2,0,1:T(2,128)}, u32[]{:S(2)}) copy-start(f32[2,262,262]{2,0,1:T(2,128)} %param.20) | copy-start | bytes 1647460
  160.2 30.7 %all-to-all-start = ((f32[16,128,128]{2,1,0:T(8,128)}), f32[16,128,128]{2,1,0:T(8,128)S(1)}, u32[]{:S(2)}, u32[]{:S(2)}) async-start(f32[16,128,128]{2,1,0:T(8,128)} %stack.2), calls=%async_computation | async-start | bytes 2097152 | tf_op jit(solution)/shard_map/all_to_all | solution.py:11
Sparse Core Ops, SparseCore 0:
  10.3 147.8 all-reduce.1
